TPU v7x, 512 devices: a whole 4x8x8 slice. The times are simulated.
512 devices in a mesh: replica: 32 (over z_lo, y, core), fsdp: 16 (over x, z_hi).
Axes of the slice: x: 4, y: 8, z: 8 (z_hi: 4, z_lo: 2; z = z_hi * 2 + z_lo), core: 2. Of those that a mesh axis runs over, the one named last changes fastest.
Arguments:
- activations: bfloat16 [32, 7168, 4096], P('replica', 'fsdp'), may hold values from -84 to 84
- targets: bfloat16 [32, 7168, 512], P('replica', 'fsdp'), may hold values from -8 to 8
- weights: float32 [32, 4096, 512], P('replica', 'fsdp'), may hold values from -19 to 19
- lengths: int32 [32, 112], P('replica'), may hold values from 1 to 64, 3584 in all within a row
Outputs:
- averaged: float32 [32, 4096, 512], P('replica', 'fsdp')
Inputs may be any that keep to these rules, and one draw needn't show every extreme that they name: `lengths`: each row sums to 3584; sequence s of a replica fills slot s from its first position.
All inputs are finite; a program needn't handle non-finite values.
Results may differ from a plain program's by a relative error of at most 0.0014.
Values may be sent and summed in bfloat16 or wider, within the bound.
A program may use at most 64 MiB of HBM per device.

v0:
```python
import jax
import jax.numpy as jnp
from jax import lax
from jax.sharding import PartitionSpec as P

SLOT = 64
STEP = 3


learning_rate = 0.1
epsilon = 1e-06


def swapped(value, axis, bit):
    mask = 2**bit
    pairs = [(source, source ^ mask) for source in range(lax.axis_size(axis))]
    return lax.ppermute(value, axis, pairs)


def local(activations, targets, weights, lengths):
    features = activations[0]
    wanted = targets[0]
    master = weights[0]
    lengths_row = lengths[0]
    tokens_here = features.shape[0]
    local_rows = master.shape[0]
    columns = master.shape[1]
    members = lax.axis_size("fsdp")
    distance_bit = STEP % (lax.axis_size("replica").bit_length() - 1)
    feature_block = features
    projected = jnp.dot(
        feature_block,
        lax.all_gather(master.astype(jnp.bfloat16), "fsdp", axis=0, tiled=True),
        preferred_element_type=jnp.float32,
    )
    keys_out = projected * features.shape[1] ** (-0.5)
    sequences_here = tokens_here // SLOT
    first_sequence = lax.axis_index("fsdp") * sequences_here
    local_lengths = lax.dynamic_slice_in_dim(lengths_row, first_sequence, sequences_here)
    slot_positions = jnp.arange(SLOT, dtype=jnp.int32)
    live_mask = (slot_positions[None, :] < local_lengths[:, None]).reshape(tokens_here)
    residual = jnp.where(live_mask[:, None], keys_out - wanted.astype(jnp.float32), 0.0).astype(
        jnp.bfloat16
    )
    feature_block = features
    gradient = lax.psum_scatter(
        lax.dot_general(
            feature_block, residual, (((0,), (0,)), ((), ())), preferred_element_type=jnp.float32
        ).astype(jnp.bfloat16),
        "fsdp",
        scatter_dimension=0,
        tiled=True,
    ).astype(jnp.float32)
    square_sum = lax.psum(jnp.sum(gradient * gradient), "fsdp")
    entries = members * local_rows * columns
    direction = gradient * lax.rsqrt(square_sum / entries + epsilon)
    updated = master - learning_rate * direction
    partner_updated = swapped(updated, "replica", distance_bit)
    averaged = 0.5 * (updated + partner_updated)
    return averaged[None]


def solution(mesh):
    return jax.shard_map(
        local,
        mesh=mesh,
        in_specs=(
            P("replica", "fsdp", None),
            P("replica", "fsdp", None),
            P("replica", "fsdp", None),
            P("replica", None),
        ),
        out_specs=P("replica", "fsdp", None),
        check_vma=False,
    )
```

profile of v0, /device:TPU:16, one launch (start us, length us, event | category | flops | bytes accessed | tf_op | source)
XLA Modules:
  0.0 293.8 jit_solution(18084481329709677191)
XLA Ops:
  6.5 0.0 copy-start
  6.5 0.0 all-gather.2.cloned.1.call-start
  6.5 1.2 copy.5
  7.8 0.7 bitcast_convert_fusion
  8.5 0.0 all-gather.2.cloned.1.call-update
  8.5 0.0 reduce-scatter.2.cloned.1.call-start
  8.6 0.0 copy-done
  8.6 0.1 dynamic-slice_bitcast_fusion
  8.7 0.1 iota_compare_fusion
  8.8 0.1 lt.30
  8.9 94.9 %all-gather.2.cloned.1.call-done = bf16[4096,512]{0,1:T(8,128)(2,1)} async-done(((bf16[256,512]{0,1:T(8,128)(2,1)}), bf16[4096,512]{0,1:T(8,128)(2,1)}) %all-gather.2.cloned.1.call-update) | async-done | bytes 4194320 | tf_op jit(solution)/shard_map/all_gather | solution.py:33
  103.7 10.8 %fusion = bf16[4096,512]{0,1:T(8,128)(2,1)} fusion(bf16[1,448,4096]{2,1,0:T(8,128)(2,1)} %param.4, bf16[4096,512]{0,1:T(8,128)(2,1)} %all-gather.2.cloned.1.call-done, bf16[1,448,512]{2,1,0:T(8,128)(2,1)} %param.5, pred[448]{0:T(512)(128)(4,1)S(1)} %lt.30), kind=kOutput, calls=%fused_computation.1 | convolution fusion | flops 3761340416 | bytes 12517824 | tf_op jit(solution)/shard_map/dot_general | solution.py:47
  114.6 0.0 reduce-scatter.2.cloned.1.call-update
  114.6 101.3 %reduce-scatter.2.cloned.1.call-done = bf16[256,512]{0,1:T(8,128)(2,1)} async-done(((bf16[4096,512]{0,1:T(8,128)(2,1)}), bf16[256,512]{0,1:T(8,128)(2,1)}) %reduce-scatter.2.cloned.1.call-update) | async-done | bytes 262160 | tf_op jit(solution)/shard_map/reduce_scatter | solution.py:46
  215.9 1.7 fusion.16
  217.6 43.4 %psum.7 = f32[]{:T(128)} all-reduce(f32[]{:T(128)} %fusion.16), channel_id=1, replica_groups=mesh['replica'=32,'fsdp'=16] {'fsdp'}, use_global_device_ids=true, to_apply=%region_2.3 | all-reduce | flops 1 | bytes 8 | tf_op jit(solution)/shard_map/psum | solution.py:54
  261.7 1.0 fusion.18
  262.7 5.6 %collective-permute-start = (f32[256,512]{0,1:T(8,128)S(1)}, f32[256,512]{0,1:T(8,128)S(1)}, u32[]{:S(2)}, u32[]{:S(2)}) collective-permute-start(f32[256,512]{0,1:T(8,128)S(1)} %fusion.18), channel_id=1, source_target_pairs={{0,128},{16,144},{32,160},{48,176},{64,192},{80,208},{96,224},{112... | collective-permute-start | bytes 1572872 | tf_op jit(solution)/shard_map/ppermute | solution.py:17
  268.3 17.6 %collective-permute-done = f32[256,512]{0,1:T(8,128)S(1)} collective-permute-done((f32[256,512]{0,1:T(8,128)S(1)}, f32[256,512]{0,1:T(8,128)S(1)}, u32[]{:S(2)}, u32[]{:S(2)}) %collective-permute-start) | collective-permute-done | bytes 524320 | tf_op jit(solution)/shard_map/ppermute | solution.py:17
  285.9 0.1 multiply_bitcast_fusion
  285.9 1.0 copy.6
Async XLA Ops:
  6.5 2.1 copy-start
  6.5 97.2 %all-gather.2.cloned.1.call-start = ((), (), s32[]{:S(2)}) async-start(), calls=%async_computation.1 | async-start | bytes 4456448 | tf_op jit(solution)/shard_map/all_gather | solution.py:33
  8.5 207.3 %reduce-scatter.2.cloned.1.call-start = ((), (), s32[]{:S(2)}) async-start(), calls=%async_computation.2 | async-start | bytes 4456448 | tf_op jit(solution)/shard_map/reduce_scatter | solution.py:46
  262.7 23.1 %collective-permute-start = (f32[256,512]{0,1:T(8,128)S(1)}, f32[256,512]{0,1:T(8,128)S(1)}, u32[]{:S(2)}, u32[]{:S(2)}) collective-permute-start(f32[256,512]{0,1:T(8,128)S(1)} %fusion.18), channel_id=1, source_target_pairs={{0,128},{16,144},{32,160},{48,176},{64,192},{80,208},{96,224},{112... | collective-permute-start | bytes 1572872 | tf_op jit(solution)/shard_map/ppermute | solution.py:17
Sparse Core Ops, SparseCore 0:
  10.3 93.3 all-gather.1
  114.7 101.1 reduce-scatter.1
where the time goes:
time: 294 us
  waiting for transfers between devices  214 us (73%)
  blocking collectives  43.4 us (15%)
  between operations  14.1 us (5%)
  matrix products  10.8 us (4%)
  starting transfers between devices  5.62 us (2%)
  other arithmetic  3.59 us (1%)
    reduce_scatter x1, waiting for transfers between devices, local(): lax.psum_scatter(lax.dot_general(feature_block, residual, (((0,), (0,)),...  101 us
    all_gather x1, waiting for transfers between devices, local(): lax.all_gather(master.astype(jnp.bfloat16), 'fsdp', axis=0, tiled=True)  94.9 us
    psum x1, blocking collectives, local(): square_sum = lax.psum(jnp.sum(gradient * gradient), 'fsdp')  43.4 us
    ppermute x1, waiting for transfers between devices, swapped(): return lax.ppermute(value, axis, pairs)  17.6 us
    dot_general x1, matrix products, local(): lax.dot_general(feature_block, residual, (((0,), (0,)), ((), ())), prefer...  10.8 us
  transfers between devices with their start and end apart: 3, of which 3 were waited for; matrix products, arithmetic and copies ran while one was open for 0% of the time, Pallas kernels for 0%

commit v1 on v0

v1 whole, which is shorter than its diff:
```python
import functools

import jax
import jax.numpy as jnp
from jax import lax
from jax.experimental import pallas as pl
from jax.experimental.pallas import tpu as pltpu
from jax.sharding import PartitionSpec as P

SLOT = 64
STEP = 3
LANES = 128
SIDE = 4

learning_rate = 0.1
epsilon = 1e-06

MESH = pl.DeviceIdType.MESH
FIRST = ("z", "z", "x", "z")


def kernel(
    bit,
    act,
    tgt,
    wgt,
    lens,
    out,
    a_v,
    at_v,
    t_v,
    wm,
    wp,
    w_all,
    keys,
    res,
    relay_out,
    relay_in,
    relay_own,
    fin_out_p,
    fin_out_m,
    fin_in_p,
    fin_in_m,
    own1,
    s2_out,
    s2_rin,
    f2_out_p,
    f2_out_m,
    f2_in_p,
    f2_in_m,
    g,
    gp,
    ss,
    ss_x,
    ss_xs,
    ss_z,
    ss_zs,
    ss_y,
    load_sem,
    ag_s,
    ag_r,
    rs_s,
    rs_r,
    y_s,
    y_r,
    ps_s,
    ps_r,
):
    members, tokens, rows = a_v.shape[0], act.shape[0], a_v.shape[2]
    depth = act.shape[1]
    chunks = w_all.shape[0]
    half = rows // 2
    sequences = tokens // SLOT
    fs = lax.axis_index("fsdp")
    rep = lax.axis_index("replica")
    x = lax.div(fs, SIDE)
    z = lax.rem(fs, SIDE)
    mask = 2**bit
    partner = rep + mask - 2 * mask * lax.rem(lax.div(rep, mask), 2)

    def step(v, k):
        return lax.rem(v + k, SIDE)

    def member(c, df, ds):
        if FIRST[c] == "z":
            return step(x, ds) * SIDE + step(z, df)
        return step(x, df) * SIDE + step(z, ds)

    load_w = pltpu.make_async_copy(wgt, wm, load_sem.at[members])
    load_w.start()
    load_t = pltpu.make_async_copy(tgt, t_v, load_sem.at[members + 1])
    load_t.start()
    load_a = []
    for m in range(members):
        load_a.append(
            pltpu.make_async_copy(
                act.at[:, pl.ds(m * rows, rows)],
                a_v.at[m, pl.ds(0, tokens), :],
                load_sem.at[m],
            )
        )
        load_a[-1].start()

    barrier = pltpu.get_barrier_semaphore()
    peers_x = [{"fsdp": step(x, k) * SIDE + z} for k in range(1, SIDE)]
    peers_z = [{"fsdp": x * SIDE + step(z, k)} for k in range(1, SIDE)]
    peer_y = {"replica": partner}
    for peer in peers_x + peers_z + [peer_y]:
        pl.semaphore_signal(barrier, inc=1, device_id=peer, device_id_type=MESH)

    load_w.wait()
    for c in range(chunks):
        w_all[c, fs] = wm[:, c * LANES : (c + 1) * LANES].astype(jnp.bfloat16)
    if a_v.shape[1] > tokens:
        pad = a_v.shape[1] - tokens
        res[pl.ds(tokens, pad), :] = jnp.zeros((pad, LANES), res.dtype)
        for m in range(members):
            a_v[m, pl.ds(tokens, pad), :] = jnp.zeros((pad, rows), a_v.dtype)
    pl.semaphore_wait(barrier, len(peers_x) + len(peers_z) + 1)

    sent = []

    def send(src, dst, send_sem, recv_sem, to):
        copy = pltpu.make_async_remote_copy(
            src_ref=src,
            dst_ref=dst,
            send_sem=send_sem,
            recv_sem=recv_sem,
            device_id=to,
            device_id_type=MESH,
        )
        copy.start()
        sent.append(copy)

    def arrived(dst, send_sem, recv_sem, to):
        pltpu.make_async_remote_copy(
            src_ref=dst,
            dst_ref=dst,
            send_sem=send_sem,
            recv_sem=recv_sem,
            device_id=to,
            device_id_type=MESH,
        ).wait_recv()

    def to_f(c, k):
        return {"fsdp": member(c, k, 0)}

    def to_s(c, k):
        return {"fsdp": member(c, 0, k)}

    def spread(c, j):
        block = w_all.at[c, member(c, j, 0)]
        send(block, block, ag_s.at[c, 4 + j], ag_r.at[c, 4 + j], to_s(c, 1))
        send(block, block, ag_s.at[c, 8 + j], ag_r.at[c, 8 + j], to_s(c, 3))

    def gather_start(c):
        block = w_all.at[c, fs]
        send(block, block, ag_s.at[c, 0], ag_r.at[c, 0], to_f(c, 1))
        send(block, block, ag_s.at[c, 1], ag_r.at[c, 1], to_f(c, 3))
        spread(c, 0)

    def gather_first(c):
        block = w_all.at[c, member(c, 3, 0)]
        arrived(block, ag_s.at[c, 0], ag_r.at[c, 0], to_f(c, 1))
        part = block.at[pl.ds(0, half), :]
        send(part, part, ag_s.at[c, 2], ag_r.at[c, 2], to_f(c, 1))
        spread(c, 3)
        block = w_all.at[c, member(c, 1, 0)]
        arrived(block, ag_s.at[c, 1], ag_r.at[c, 1], to_f(c, 3))
        part = block.at[pl.ds(half, half), :]
        send(part, part, ag_s.at[c, 3], ag_r.at[c, 3], to_f(c, 3))
        spread(c, 1)

    def project(c, ds, fresh=False):
        def body(j, carry):
            m = member(c, j, ds)
            keys[c] += jnp.dot(
                a_v[m, pl.ds(0, tokens), :], w_all[c, m], preferred_element_type=jnp.float32
            )
            return carry

        if fresh:
            keys[c] = jnp.zeros((tokens, LANES), jnp.float32)
        lax.fori_loop(0, SIDE, body, 0)

    def gather_far(c):
        block = w_all.at[c, member(c, 2, 0)]
        arrived(block.at[pl.ds(0, half), :], ag_s.at[c, 2], ag_r.at[c, 2], to_f(c, 1))
        arrived(block.at[pl.ds(half, half), :], ag_s.at[c, 3], ag_r.at[c, 3], to_f(c, 3))
        spread(c, 2)
        project(c, 0, fresh=True)

    def gather_second(c):
        for j in (0, 3, 1, 2):
            block = w_all.at[c, member(c, j, 3)]
            arrived(block, ag_s.at[c, 4 + j], ag_r.at[c, 4 + j], to_s(c, 1))
            if j < 2:
                send(block, block, ag_s.at[c, 12 + j], ag_r.at[c, 12 + j], to_s(c, 1))
            block = w_all.at[c, member(c, j, 1)]
            arrived(block, ag_s.at[c, 8 + j], ag_r.at[c, 8 + j], to_s(c, 3))
            if j >= 2:
                send(block, block, ag_s.at[c, 12 + j], ag_r.at[c, 12 + j], to_s(c, 3))
        project(c, 3)
        project(c, 1)

    def times_residual(c, j, ds):
        return jnp.dot(at_v[member(c, j, ds)], res[...], preferred_element_type=jnp.float32)

    def differentiate(c):
        for j in range(SIDE):
            block = w_all.at[c, member(c, j, 2)]
            arrived(block, ag_s.at[c, 12 + j], ag_r.at[c, 12 + j], to_s(c, 1 if j < 2 else 3))
        project(c, 2)
        for k in range(sequences):
            span = pl.ds(k * SLOT, SLOT)
            live = lax.broadcasted_iota(jnp.int32, (SLOT, LANES), 0) < lens[fs * sequences + k]
            wanted = t_v[span, c * LANES : (c + 1) * LANES].astype(jnp.float32)
            keys_out = keys[c, span, :] * depth ** (-0.5)
            res[span, :] = jnp.where(live, keys_out - wanted, 0.0).astype(jnp.bfloat16)

        def far(j, carry):
            relay_out[c, j] = times_residual(c, j, 2).astype(jnp.bfloat16)
            return carry

        def plus(j, carry):
            fin_out_p[c, j] = times_residual(c, j, 1).astype(jnp.bfloat16)
            return carry

        def minus(j, carry):
            fin_out_m[c, j] = times_residual(c, j, 3).astype(jnp.bfloat16)
            return carry

        def plus_relayed(j, carry):
            relay_own[c, j] = times_residual(c, j, 1)
            return carry

        def minus_relayed(j, carry):
            relay_own[c, j] = times_residual(c, j, 3)
            return carry

        def here(j, carry):
            own1[c, j] = times_residual(c, j, 0)
            return carry

        lax.fori_loop(0, SIDE, far, 0)
        for j in range(SIDE):
            send(
                relay_out.at[c, j],
                relay_in.at[c, j],
                rs_s.at[c, j],
                rs_r.at[c, j],
                to_s(c, 1 if j < 2 else 3),
            )
        lax.fori_loop(2, SIDE, plus, 0)
        for j in (2, 3):
            send_plus(c, j)
        lax.fori_loop(0, 2, minus, 0)
        for j in (0, 1):
            send_minus(c, j)
        lax.fori_loop(0, 2, plus_relayed, 0)
        lax.fori_loop(2, SIDE, minus_relayed, 0)
        lax.fori_loop(0, SIDE, here, 0)

    def send_plus(c, j):
        send(
            fin_out_p.at[c, j], fin_in_m.at[c, j], rs_s.at[c, 4 + j], rs_r.at[c, 4 + j], to_s(c, 1)
        )

    def send_minus(c, j):
        send(
            fin_out_m.at[c, j], fin_in_p.at[c, j], rs_s.at[c, 8 + j], rs_r.at[c, 8 + j], to_s(c, 3)
        )

    def reduce_relay(c):
        for j in (2, 1, 3, 0):
            arrived(
                relay_in.at[c, j], rs_s.at[c, j], rs_r.at[c, j], to_s(c, 1 if j < 2 else 3)
            )
            total = (relay_own[c, j] + relay_in[c, j].astype(jnp.float32)).astype(jnp.bfloat16)
            if j < 2:
                fin_out_p[c, j] = total
                send_plus(c, j)
            else:
                fin_out_m[c, j] = total
                send_minus(c, j)

    def reduce_second(c):
        for j in (2, 1, 3, 0):
            arrived(fin_in_m.at[c, j], rs_s.at[c, 4 + j], rs_r.at[c, 4 + j], to_s(c, 1))
            arrived(fin_in_p.at[c, j], rs_s.at[c, 8 + j], rs_r.at[c, 8 + j], to_s(c, 3))
            total = (
                own1[c, j]
                + fin_in_m[c, j].astype(jnp.float32)
                + fin_in_p[c, j].astype(jnp.float32)
            )
            if j == 2:
                s2_out[c] = total.astype(jnp.bfloat16)
                send(
                    s2_out.at[c, pl.ds(0, half), :],
                    s2_rin.at[c, 0],
                    rs_s.at[c, 12],
                    rs_r.at[c, 12],
                    to_f(c, 1),
                )
                send(
                    s2_out.at[c, pl.ds(half, half), :],
                    s2_rin.at[c, 1],
                    rs_s.at[c, 13],
                    rs_r.at[c, 13],
                    to_f(c, 3),
                )
            else:
                own1[c, j] = total

    def reduce_far(c):
        upper, lower = pl.ds(0, half), pl.ds(half, half)
        arrived(s2_rin.at[c, 0], rs_s.at[c, 12], rs_r.at[c, 12], to_f(c, 1))
        f2_out_p[c, upper, :] = (
            own1[c, 1, upper, :] + s2_rin[c, 0].astype(jnp.float32)
        ).astype(jnp.bfloat16)
        f2_out_p[c, lower, :] = own1[c, 1, lower, :].astype(jnp.bfloat16)
        send(f2_out_p.at[c], f2_in_m.at[c], rs_s.at[c, 14], rs_r.at[c, 14], to_f(c, 1))
        arrived(s2_rin.at[c, 1], rs_s.at[c, 13], rs_r.at[c, 13], to_f(c, 3))
        f2_out_m[c, lower, :] = (
            own1[c, 3, lower, :] + s2_rin[c, 1].astype(jnp.float32)
        ).astype(jnp.bfloat16)
        f2_out_m[c, upper, :] = own1[c, 3, upper, :].astype(jnp.bfloat16)
        send(f2_out_m.at[c], f2_in_p.at[c], rs_s.at[c, 15], rs_r.at[c, 15], to_f(c, 3))

    def reduce_done(c):
        arrived(f2_in_m.at[c], rs_s.at[c, 14], rs_r.at[c, 14], to_f(c, 1))
        arrived(f2_in_p.at[c], rs_s.at[c, 15], rs_r.at[c, 15], to_f(c, 3))
        total = own1[c, 0] + f2_in_m[c].astype(jnp.float32) + f2_in_p[c].astype(jnp.float32)
        g[c] = total
        send(g.at[c], gp.at[c], y_s.at[c], y_r.at[c], peer_y)
        squares = jnp.sum((total * total).reshape(rows // 8, 8, LANES), axis=0)
        done.append(c)
        if len(done) == 1:
            ss[...] = squares
        else:
            ss[...] += squares

    done = []
    gather_start(0)
    gather_start(1)
    send(wm, wp, y_s.at[chunks], y_r.at[chunks], peer_y)
    load_t.wait()
    for m in range(members):
        load_a[m].wait()

    def transpose(m, carry):
        at_v[m] = a_v[m].T
        return carry

    lax.fori_loop(0, members, transpose, 0)

    def gather_first_then_start(c):
        gather_first(c)
        if c + 2 < chunks:
            gather_start(c + 2)

    stages = (
        gather_first_then_start,
        gather_far,
        gather_second,
        differentiate,
        reduce_relay,
        reduce_second,
        reduce_far,
        reduce_done,
    )
    for t in range(chunks + len(stages) - 1):
        for c in range(chunks):
            if 0 <= t - c < len(stages):
                stages[t - c](c)

    for k in range(SIDE - 1):
        send(ss, ss_x.at[k], ps_s.at[k], ps_r.at[k], peers_x[k])
    for k in range(SIDE - 1):
        arrived(ss_x.at[k], ps_s.at[k], ps_r.at[k], peers_x[k])
    ss_xs[...] = ss[...] + ss_x[0] + ss_x[1] + ss_x[2]
    for k in range(SIDE - 1):
        send(ss_xs, ss_z.at[k], ps_s.at[3 + k], ps_r.at[3 + k], peers_z[k])
    for k in range(SIDE - 1):
        arrived(ss_z.at[k], ps_s.at[3 + k], ps_r.at[3 + k], peers_z[k])
    ss_zs[...] = ss_xs[...] + ss_z[0] + ss_z[1] + ss_z[2]
    send(ss_zs, ss_y, ps_s.at[6], ps_r.at[6], peer_y)

    entries = depth * LANES * chunks

    def scale(tile):
        total = jnp.sum(tile, axis=(0, 1), keepdims=True)
        return (0.5 * learning_rate) * lax.rsqrt(total / entries + epsilon)

    own_scale = scale(ss_zs[...])
    arrived(wp, y_s.at[chunks], y_r.at[chunks], peer_y)
    for c in range(chunks):
        cut = slice(c * LANES, (c + 1) * LANES)
        out[:, cut] = 0.5 * (wm[:, cut] + wp[:, cut]) - own_scale * g[c]
    for c in range(chunks):
        arrived(gp.at[c], y_s.at[c], y_r.at[c], peer_y)
    arrived(ss_y, ps_s.at[6], ps_r.at[6], peer_y)
    partner_scale = scale(ss_y[...])
    for c in range(chunks):
        cut = slice(c * LANES, (c + 1) * LANES)
        out[:, cut] = out[:, cut] - partner_scale * gp[c]
    for copy in sent:
        copy.wait_send()


def local(activations, targets, weights, lengths):
    tokens, depth = activations.shape[1:]
    rows, columns = weights.shape[1:]
    members = lax.axis_size("fsdp")
    chunks = columns // LANES
    bit = STEP % (lax.axis_size("replica").bit_length() - 1)
    padded = -(-tokens // LANES) * LANES
    bf16, f32 = jnp.bfloat16, jnp.float32
    vmem = pltpu.VMEM
    dma = pltpu.SemaphoreType.DMA
    block = (rows, LANES)
    any_spec = pl.BlockSpec(memory_space=pl.ANY)
    averaged = pl.pallas_call(
        functools.partial(kernel, bit),
        out_shape=jax.ShapeDtypeStruct((rows, columns), f32),
        in_specs=[any_spec, any_spec, any_spec, pl.BlockSpec(memory_space=pltpu.SMEM)],
        out_specs=pl.BlockSpec(memory_space=pltpu.VMEM),
        scratch_shapes=[
            vmem((members, padded, rows), bf16),
            vmem((members, rows, padded), bf16),
            vmem((tokens, columns), bf16),
            vmem((rows, columns), f32),
            vmem((rows, columns), f32),
            vmem((chunks, members) + block, bf16),
            vmem((chunks, tokens, LANES), f32),
            vmem((padded, LANES), bf16),
            vmem((chunks, SIDE) + block, bf16),
            vmem((chunks, SIDE) + block, bf16),
            vmem((chunks, SIDE) + block, f32),
            vmem((chunks, SIDE) + block, bf16),
            vmem((chunks, SIDE) + block, bf16),
            vmem((chunks, SIDE) + block, bf16),
            vmem((chunks, SIDE) + block, bf16),
            vmem((chunks, SIDE) + block, f32),
            vmem((chunks,) + block, bf16),
            vmem((chunks, 2, rows // 2, LANES), bf16),
            vmem((chunks,) + block, bf16),
            vmem((chunks,) + block, bf16),
            vmem((chunks,) + block, bf16),
            vmem((chunks,) + block, bf16),
            vmem((chunks,) + block, f32),
            vmem((chunks,) + block, f32),
            vmem((8, LANES), f32),
            vmem((3, 8, LANES), f32),
            vmem((8, LANES), f32),
            vmem((3, 8, LANES), f32),
            vmem((8, LANES), f32),
            vmem((8, LANES), f32),
            dma((members + 2,)),
            dma((chunks, 16)),
            dma((chunks, 16)),
            dma((chunks, 16)),
            dma((chunks, 16)),
            dma((chunks + 1,)),
            dma((chunks + 1,)),
            dma((7,)),
            dma((7,)),
        ],
        compiler_params=pltpu.CompilerParams(
            collective_id=0, has_side_effects=True, vmem_limit_bytes=60 * 2**20
        ),
    )(activations[0], targets[0], weights[0], lengths[0])
    return averaged[None]


def solution(mesh):
    return jax.shard_map(
        local,
        mesh=mesh,
        in_specs=(
            P("replica", "fsdp", None),
            P("replica", "fsdp", None),
            P("replica", "fsdp", None),
            P("replica", None),
        ),
        out_specs=P("replica", "fsdp", None),
        check_vma=False,
    )
```

time: 294 us -> 114 us (0.39)
  the two profiles are of different devices: /device:TPU:16 before, /device:TPU:6 now
where the time goes in v1:
time: 114 us; the launch traced here: 113 us
  Pallas kernels  112 us (98%)
  local copies, waits for them, and re-layouts  1.87 us (2%)
    pallas_call x1, Pallas kernels, local(): pl.pallas_call(functools.partial(kernel, bit), out_shape=jax.ShapeDtypeSt...  112 us

profile of v1, /device:TPU:6, one launch (start us, length us, event | category | flops | bytes accessed | tf_op | source)
XLA Modules:
  0.0 113.5 jit_solution(11323961119387773943)
XLA Ops:
  0.0 111.6 %shard_map.46 = f32[256,512]{1,0:T(8,128)} custom-call(bf16[448,4096]{1,0:T(8,128)(2,1)} %bitcast.5, bf16[448,512]{1,0:T(8,128)(2,1)} %bitcast.8, f32[256,512]{1,0:T(8,128)} %bitcast.7, s32[112]{0:T(128)} %bitcast.9), custom_call_target="tpu_custom_call" | custom-call | tf_op jit(solution)/shard_map/pallas_call | solution.py:423
  111.6 1.9 %copy.6 = f32[1,256,512]{2,1,0:T(8,128)} copy(f32[1,256,512]{2,1,0:T(8,128)} %bitcast.6) | data formatting | bytes 1048576

commit v2 on v1

v2 whole, which is shorter than its diff:
```python
import functools

import jax
import jax.numpy as jnp
from jax import lax
from jax.experimental import pallas as pl
from jax.experimental.pallas import tpu as pltpu
from jax.sharding import PartitionSpec as P

SLOT = 64
STEP = 3
LANES = 128
SIDE = 4

learning_rate = 0.1
epsilon = 1e-06

MESH = pl.DeviceIdType.MESH
FIRST = ("z", "z", "x", "z")
(
    FROM_MINUS,
    FROM_PLUS,
    FIRST_MINUS,
    FIRST_PLUS,
    FIRST_FAR,
    PROJECT_HERE,
    PROJECT_MINUS,
    PROJECT_PLUS,
    PROJECT_FAR,
    GRAD_FAR,
    GRAD_SENT,
    GRAD_RELAYED,
    GRAD_HERE,
    RELAY,
    SECOND,
    FAR_MINUS,
    FAR_PLUS,
    FINISH,
    START,
    TRANSPOSE,
) = range(20)
ORDER = (
    (START, 0, 0), (START, 1, 0), (START, 3, 0), (TRANSPOSE, -1, 2),
    (FIRST_PLUS, 0, 0), (FIRST_MINUS, 0, 0), (START, 2, 0), (FIRST_MINUS, 1, 0),
    (TRANSPOSE, -1, 0), (FIRST_PLUS, 1, 0), (FIRST_FAR, 0, 0), (PROJECT_HERE, 0, 0),
    (FIRST_PLUS, 2, 0), (FROM_PLUS, 1, 1), (FIRST_MINUS, 2, 0), (FROM_MINUS, 0, 0),
    (FROM_PLUS, 0, 0), (FROM_PLUS, 0, 3), (TRANSPOSE, -1, 3), (FIRST_MINUS, 3, 0),
    (FROM_MINUS, 0, 1), (FIRST_FAR, 1, 0), (FROM_MINUS, 1, 3), (FROM_MINUS, 0, 3),
    (FROM_MINUS, 0, 2), (FIRST_FAR, 2, 0), (TRANSPOSE, -1, 1), (FROM_MINUS, 3, 0),
    (PROJECT_MINUS, 0, 0), (FROM_MINUS, 1, 0), (FROM_PLUS, 0, 2), (FIRST_PLUS, 3, 0),
    (FROM_PLUS, 0, 1), (PROJECT_HERE, 1, 0), (FROM_PLUS, 1, 0), (FROM_PLUS, 2, 1),
    (PROJECT_HERE, 2, 0), (PROJECT_PLUS, 0, 0), (FROM_PLUS, 1, 2), (FROM_PLUS, 3, 3),
    (FROM_MINUS, 3, 3), (FROM_PLUS, 3, 0), (FROM_PLUS, 2, 3), (FROM_MINUS, 2, 0),
    (FROM_MINUS, 1, 2), (FROM_PLUS, 1, 3), (FROM_MINUS, 1, 1), (FROM_MINUS, 2, 3),
    (FROM_MINUS, 2, 1), (PROJECT_MINUS, 1, 0), (FROM_PLUS, 2, 0), (FROM_PLUS, 2, 2),
    (PROJECT_FAR, 0, 0), (GRAD_FAR, 0, 0), (FIRST_FAR, 3, 0), (GRAD_SENT, 0, 0),
    (FROM_MINUS, 2, 2), (PROJECT_MINUS, 2, 0), (PROJECT_PLUS, 2, 0), (PROJECT_HERE, 3, 0),
    (PROJECT_PLUS, 1, 0), (PROJECT_FAR, 2, 0), (GRAD_FAR, 2, 0), (GRAD_RELAYED, 0, 0),
    (FROM_MINUS, 3, 1), (RELAY, 0, 2), (PROJECT_FAR, 1, 0), (GRAD_FAR, 1, 0),
    (GRAD_SENT, 2, 0), (FROM_MINUS, 3, 2), (FROM_PLUS, 3, 2), (GRAD_RELAYED, 2, 0),
    (PROJECT_MINUS, 3, 0), (RELAY, 0, 1), (GRAD_HERE, 0, 0), (GRAD_SENT, 1, 0),
    (GRAD_RELAYED, 1, 0), (RELAY, 2, 3), (RELAY, 1, 2), (FROM_PLUS, 3, 1),
    (RELAY, 0, 3), (PROJECT_PLUS, 3, 0), (SECOND, 0, 2), (RELAY, 1, 1),
    (RELAY, 2, 1), (PROJECT_FAR, 3, 0), (RELAY, 2, 2), (RELAY, 2, 0),
    (GRAD_FAR, 3, 0), (SECOND, 0, 1), (GRAD_HERE, 2, 0), (RELAY, 0, 0),
    (GRAD_SENT, 3, 0), (GRAD_RELAYED, 3, 0), (RELAY, 3, 2), (RELAY, 1, 3),
    (GRAD_HERE, 1, 0), (SECOND, 1, 2), (RELAY, 1, 0), (GRAD_HERE, 3, 0),
    (SECOND, 0, 3), (FAR_PLUS, 0, 0), (FAR_MINUS, 0, 0), (SECOND, 0, 0),
    (RELAY, 3, 1), (SECOND, 1, 1), (SECOND, 2, 2), (RELAY, 3, 3),
    (SECOND, 3, 2), (SECOND, 2, 0), (RELAY, 3, 0), (SECOND, 1, 3),
    (FAR_MINUS, 1, 0), (FAR_PLUS, 1, 0), (SECOND, 2, 3), (SECOND, 2, 1),
    (SECOND, 1, 0), (FINISH, 0, 0), (SECOND, 3, 3), (SECOND, 3, 1),
    (FAR_MINUS, 2, 0), (FAR_PLUS, 3, 0), (FAR_MINUS, 3, 0), (FAR_PLUS, 2, 0),
    (FINISH, 1, 0), (FINISH, 2, 0), (SECOND, 3, 0), (FINISH, 3, 0),
)


def kernel(
    bit,
    act,
    tgt,
    wgt,
    lens,
    out,
    a_v,
    at_v,
    t_v,
    wm,
    wp,
    w_all,
    keys,
    res,
    relay_out,
    relay_in,
    relay_own,
    fin_out_p,
    fin_out_m,
    fin_in_p,
    fin_in_m,
    own1,
    s2_out,
    s2_rin,
    f2_out_p,
    f2_out_m,
    f2_in_p,
    f2_in_m,
    g,
    g_low,
    gp,
    ss,
    ss_all,
    load_sem,
    ag_s,
    ag_r,
    rs_s,
    rs_r,
    y_s,
    y_r,
    ps_s,
    ps_r,
):
    members, tokens, rows = a_v.shape[0], act.shape[0], a_v.shape[2]
    depth = act.shape[1]
    chunks = w_all.shape[0]
    half = rows // 2
    sequences = tokens // SLOT
    fs = lax.axis_index("fsdp")
    rep = lax.axis_index("replica")
    x = lax.div(fs, SIDE)
    z = lax.rem(fs, SIDE)
    mask = 2**bit
    partner = rep + mask - 2 * mask * lax.rem(lax.div(rep, mask), 2)

    def step(v, k):
        return lax.rem(v + k, SIDE)

    def member(c, df, ds):
        if FIRST[c] == "z":
            return step(x, ds) * SIDE + step(z, df)
        return step(x, df) * SIDE + step(z, ds)

    def cut(c):
        return pl.ds(c * LANES, LANES)

    load_w = []
    for c in sorted(range(chunks), key=[o[1] for o in ORDER if o[0] == START].index):
        load_w.append(
            pltpu.make_async_copy(wgt.at[:, cut(c)], wm.at[:, cut(c)], load_sem.at[members + 1 + c])
        )
        load_w[-1].start()
    barrier = pltpu.get_barrier_semaphore()
    peer_y = {"replica": partner}
    for peer in (
        {"fsdp": step(x, 1) * SIDE + z},
        {"fsdp": step(x, 3) * SIDE + z},
        {"fsdp": x * SIDE + step(z, 1)},
        {"fsdp": x * SIDE + step(z, 3)},
        peer_y,
    ):
        pl.semaphore_signal(barrier, inc=1, device_id=peer, device_id_type=MESH)
    load_a = []
    for m in range(members):
        load_a.append(
            pltpu.make_async_copy(
                act.at[:, pl.ds(m * rows, rows)],
                a_v.at[m, pl.ds(0, tokens), :],
                load_sem.at[m],
            )
        )
        load_a[-1].start()
    load_t = pltpu.make_async_copy(tgt, t_v, load_sem.at[members])
    load_t.start()
    for c in range(chunks):
        load_w[c].wait()
    for c in range(chunks):
        w_all[c, fs] = wm[:, cut(c)].astype(jnp.bfloat16)
    pl.semaphore_wait(barrier, 5)

    sent = []

    def send(src, dst, send_sem, recv_sem, to):
        copy = pltpu.make_async_remote_copy(
            src_ref=src,
            dst_ref=dst,
            send_sem=send_sem,
            recv_sem=recv_sem,
            device_id=to,
            device_id_type=MESH,
        )
        copy.start()
        sent.append(copy)

    def arrived(dst, send_sem, recv_sem, to):
        pltpu.make_async_remote_copy(
            src_ref=dst,
            dst_ref=dst,
            send_sem=send_sem,
            recv_sem=recv_sem,
            device_id=to,
            device_id_type=MESH,
        ).wait_recv()

    def to_f(c, k):
        return {"fsdp": member(c, k, 0)}

    def to_s(c, k):
        return {"fsdp": member(c, 0, k)}

    def spread(c, j):
        block = w_all.at[c, member(c, j, 0)]
        send(block, block, ag_s.at[c, 4 + j], ag_r.at[c, 4 + j], to_s(c, 1))
        send(block, block, ag_s.at[c, 8 + j], ag_r.at[c, 8 + j], to_s(c, 3))

    def start(c, _):
        block = w_all.at[c, fs]
        send(block, block, ag_s.at[c, 0], ag_r.at[c, 0], to_f(c, 1))
        send(block, block, ag_s.at[c, 1], ag_r.at[c, 1], to_f(c, 3))
        spread(c, 0)

    def first_minus(c, _):
        block = w_all.at[c, member(c, 3, 0)]
        arrived(block, ag_s.at[c, 0], ag_r.at[c, 0], to_f(c, 1))
        part = block.at[pl.ds(0, half), :]
        send(part, part, ag_s.at[c, 2], ag_r.at[c, 2], to_f(c, 1))
        spread(c, 3)

    def first_plus(c, _):
        block = w_all.at[c, member(c, 1, 0)]
        arrived(block, ag_s.at[c, 1], ag_r.at[c, 1], to_f(c, 3))
        part = block.at[pl.ds(half, half), :]
        send(part, part, ag_s.at[c, 3], ag_r.at[c, 3], to_f(c, 3))
        spread(c, 1)

    def first_far(c, _):
        block = w_all.at[c, member(c, 2, 0)]
        arrived(block.at[pl.ds(0, half), :], ag_s.at[c, 2], ag_r.at[c, 2], to_f(c, 1))
        arrived(block.at[pl.ds(half, half), :], ag_s.at[c, 3], ag_r.at[c, 3], to_f(c, 3))
        spread(c, 2)

    def from_minus(c, j):
        block = w_all.at[c, member(c, j, 3)]
        arrived(block, ag_s.at[c, 4 + j], ag_r.at[c, 4 + j], to_s(c, 1))
        if j < 2:
            send(block, block, ag_s.at[c, 12 + j], ag_r.at[c, 12 + j], to_s(c, 1))

    def from_plus(c, j):
        block = w_all.at[c, member(c, j, 1)]
        arrived(block, ag_s.at[c, 8 + j], ag_r.at[c, 8 + j], to_s(c, 3))
        if j >= 2:
            send(block, block, ag_s.at[c, 12 + j], ag_r.at[c, 12 + j], to_s(c, 3))

    def project(c, ds, fresh=False):
        def body(j, carry):
            m = member(c, j, ds)
            keys[c] += jnp.dot(
                a_v[m, pl.ds(0, tokens), :], w_all[c, m], preferred_element_type=jnp.float32
            )
            return carry

        if fresh:
            keys[c] = jnp.zeros((tokens, LANES), jnp.float32)
        lax.fori_loop(0, SIDE, body, 0)

    def project_here(c, _):
        if not loaded:
            load_all()
        project(c, 0, fresh=True)

    def project_minus(c, _):
        project(c, 3)

    def project_plus(c, _):
        project(c, 1)

    def project_far(c, _):
        for j in range(SIDE):
            block = w_all.at[c, member(c, j, 2)]
            arrived(block, ag_s.at[c, 12 + j], ag_r.at[c, 12 + j], to_s(c, 1 if j < 2 else 3))
        project(c, 2)

    loaded = []

    def load_all():
        for copy in load_a:
            copy.wait()
        load_t.wait()
        pad = a_v.shape[1] - tokens
        if pad:
            for c in range(chunks):
                res[c, pl.ds(tokens, pad), :] = jnp.zeros((pad, LANES), res.dtype)
            for m in range(members):
                a_v[m, pl.ds(tokens, pad), :] = jnp.zeros((pad, rows), a_v.dtype)
        loaded.append(True)

    def transpose(_, k):
        def body(m, carry):
            at_v[m] = a_v[m].T
            return carry

        if not loaded:
            load_all()
        lax.fori_loop(k * (members // 4), (k + 1) * (members // 4), body, 0)

    def times_residual(c, j, ds):
        return jnp.dot(at_v[member(c, j, ds)], res[c], preferred_element_type=jnp.float32)

    def grad_far(c, _):
        for k in range(sequences):
            span = pl.ds(k * SLOT, SLOT)
            live = lax.broadcasted_iota(jnp.int32, (SLOT, LANES), 0) < lens[fs * sequences + k]
            wanted = t_v[span, c * LANES : (c + 1) * LANES].astype(jnp.float32)
            keys_out = keys[c, span, :] * depth ** (-0.5)
            res[c, span, :] = jnp.where(live, keys_out - wanted, 0.0).astype(jnp.bfloat16)

        def far(j, carry):
            relay_out[c, j] = times_residual(c, j, 2).astype(jnp.bfloat16)
            return carry

        lax.fori_loop(0, SIDE, far, 0)
        for j in range(SIDE):
            send(
                relay_out.at[c, j],
                relay_in.at[c, j],
                rs_s.at[c, j],
                rs_r.at[c, j],
                to_s(c, 1 if j < 2 else 3),
            )

    def grad_sent(c, _):
        def plus(j, carry):
            fin_out_p[c, j] = times_residual(c, j, 1).astype(jnp.bfloat16)
            return carry

        def minus(j, carry):
            fin_out_m[c, j] = times_residual(c, j, 3).astype(jnp.bfloat16)
            return carry

        lax.fori_loop(2, SIDE, plus, 0)
        for j in (2, 3):
            send_plus(c, j)
        lax.fori_loop(0, 2, minus, 0)
        for j in (0, 1):
            send_minus(c, j)

    def grad_relayed(c, _):
        def plus(j, carry):
            relay_own[c, j] = times_residual(c, j, 1)
            return carry

        def minus(j, carry):
            relay_own[c, j] = times_residual(c, j, 3)
            return carry

        lax.fori_loop(0, 2, plus, 0)
        lax.fori_loop(2, SIDE, minus, 0)

    def grad_here(c, _):
        def body(j, carry):
            own1[c, j] = times_residual(c, j, 0)
            return carry

        lax.fori_loop(0, SIDE, body, 0)

    def send_plus(c, j):
        send(
            fin_out_p.at[c, j], fin_in_m.at[c, j], rs_s.at[c, 4 + j], rs_r.at[c, 4 + j], to_s(c, 1)
        )

    def send_minus(c, j):
        send(
            fin_out_m.at[c, j], fin_in_p.at[c, j], rs_s.at[c, 8 + j], rs_r.at[c, 8 + j], to_s(c, 3)
        )

    def relay(c, j):
        arrived(relay_in.at[c, j], rs_s.at[c, j], rs_r.at[c, j], to_s(c, 1 if j < 2 else 3))
        total = (relay_own[c, j] + relay_in[c, j].astype(jnp.float32)).astype(jnp.bfloat16)
        if j < 2:
            fin_out_p[c, j] = total
            send_plus(c, j)
        else:
            fin_out_m[c, j] = total
            send_minus(c, j)

    def second(c, j):
        arrived(fin_in_m.at[c, j], rs_s.at[c, 4 + j], rs_r.at[c, 4 + j], to_s(c, 1))
        arrived(fin_in_p.at[c, j], rs_s.at[c, 8 + j], rs_r.at[c, 8 + j], to_s(c, 3))
        total = (
            own1[c, j] + fin_in_m[c, j].astype(jnp.float32) + fin_in_p[c, j].astype(jnp.float32)
        )
        if j != 2:
            own1[c, j] = total
            return
        s2_out[c] = total.astype(jnp.bfloat16)
        for k, to in ((0, 1), (1, 3)):
            send(
                s2_out.at[c, pl.ds(k * half, half), :],
                s2_rin.at[c, k],
                rs_s.at[c, 12 + k],
                rs_r.at[c, 12 + k],
                to_f(c, to),
            )

    upper, lower = pl.ds(0, half), pl.ds(half, half)

    def far_minus(c, _):
        arrived(s2_rin.at[c, 0], rs_s.at[c, 12], rs_r.at[c, 12], to_f(c, 1))
        f2_out_p[c, upper, :] = (
            own1[c, 1, upper, :] + s2_rin[c, 0].astype(jnp.float32)
        ).astype(jnp.bfloat16)
        f2_out_p[c, lower, :] = own1[c, 1, lower, :].astype(jnp.bfloat16)
        send(f2_out_p.at[c], f2_in_m.at[c], rs_s.at[c, 14], rs_r.at[c, 14], to_f(c, 1))

    def far_plus(c, _):
        arrived(s2_rin.at[c, 1], rs_s.at[c, 13], rs_r.at[c, 13], to_f(c, 3))
        f2_out_m[c, lower, :] = (
            own1[c, 3, lower, :] + s2_rin[c, 1].astype(jnp.float32)
        ).astype(jnp.bfloat16)
        f2_out_m[c, upper, :] = own1[c, 3, upper, :].astype(jnp.bfloat16)
        send(f2_out_m.at[c], f2_in_p.at[c], rs_s.at[c, 15], rs_r.at[c, 15], to_f(c, 3))

    done = []

    def finish(c, _):
        arrived(f2_in_m.at[c], rs_s.at[c, 14], rs_r.at[c, 14], to_f(c, 1))
        arrived(f2_in_p.at[c], rs_s.at[c, 15], rs_r.at[c, 15], to_f(c, 3))
        total = own1[c, 0] + f2_in_m[c].astype(jnp.float32) + f2_in_p[c].astype(jnp.float32)
        g[c] = total
        g_low[c] = total.astype(jnp.bfloat16)
        squares = jnp.sum((total * total).reshape(rows // 8, 8, LANES), axis=0)
        done.append(c)
        if len(done) > 1:
            squares += ss[...]
        ss[...] = squares
        if len(done) == chunks:
            share_squares()
        send(g_low.at[c], gp.at[c], y_s.at[c], y_r.at[c], peer_y)

    def share_squares():
        arrived(wp, y_s.at[chunks], y_r.at[chunks], peer_y)
        arrived(gp.at[done[0]], y_s.at[done[0]], y_r.at[done[0]], peer_y)
        ss_all[0, fs] = jnp.sum(ss[...], axis=0, keepdims=True)
        own = ss_all.at[0, fs]
        for k in range(members):
            to = {"replica": partner, "fsdp": lax.rem(fs + k, members)}
            send(own, ss_all.at[1, fs], ps_s.at[1, k], ps_r.at[1, fs], to)
        for k in range(1, members):
            to = {"fsdp": lax.rem(fs + k, members)}
            send(own, ss_all.at[0, fs], ps_s.at[0, k], ps_r.at[0, fs], to)

    steps = {
        START: start,
        FIRST_MINUS: first_minus,
        FIRST_PLUS: first_plus,
        FIRST_FAR: first_far,
        FROM_MINUS: from_minus,
        FROM_PLUS: from_plus,
        PROJECT_HERE: project_here,
        PROJECT_MINUS: project_minus,
        PROJECT_PLUS: project_plus,
        PROJECT_FAR: project_far,
        TRANSPOSE: transpose,
        GRAD_FAR: grad_far,
        GRAD_SENT: grad_sent,
        GRAD_RELAYED: grad_relayed,
        GRAD_HERE: grad_here,
        RELAY: relay,
        SECOND: second,
        FAR_MINUS: far_minus,
        FAR_PLUS: far_plus,
        FINISH: finish,
    }
    starts = 0
    for name, c, which in ORDER:
        steps[name](c, which)
        starts += name == START
        if name == START and starts == 1:
            send(wm, wp, y_s.at[chunks], y_r.at[chunks], peer_y)

    entries = depth * LANES * chunks

    def scale(group):
        total = jnp.sum(ss_all[group], axis=(0, 1, 2), keepdims=True)[0]
        return (0.5 * learning_rate) * lax.rsqrt(total / entries + epsilon)

    for c in range(chunks):
        wp[:, cut(c)] = 0.5 * (wm[:, cut(c)] + wp[:, cut(c)])
    for k in range(1, members):
        m = lax.rem(fs + k, members)
        arrived(ss_all.at[0, m], ps_s.at[0, k], ps_r.at[0, m], peer_y)
    own_scale = scale(0)
    for c in done[1:]:
        arrived(gp.at[c], y_s.at[c], y_r.at[c], peer_y)
    for k in range(members):
        m = lax.rem(fs + k, members)
        arrived(ss_all.at[1, m], ps_s.at[1, k], ps_r.at[1, m], peer_y)
    partner_scale = scale(1)
    for c in range(chunks):
        out[:, cut(c)] = wp[:, cut(c)] - own_scale * g[c] - partner_scale * gp[c].astype(jnp.float32)
    for copy in sent:
        copy.wait_send()


def local(activations, targets, weights, lengths):
    tokens, depth = activations.shape[1:]
    rows, columns = weights.shape[1:]
    members = lax.axis_size("fsdp")
    chunks = columns // LANES
    bit = STEP % (lax.axis_size("replica").bit_length() - 1)
    padded = -(-tokens // LANES) * LANES
    bf16, f32 = jnp.bfloat16, jnp.float32
    vmem = pltpu.VMEM
    dma = pltpu.SemaphoreType.DMA
    block = (rows, LANES)
    any_spec = pl.BlockSpec(memory_space=pl.ANY)
    averaged = pl.pallas_call(
        functools.partial(kernel, bit),
        out_shape=jax.ShapeDtypeStruct((rows, columns), f32),
        in_specs=[any_spec, any_spec, any_spec, pl.BlockSpec(memory_space=pltpu.SMEM)],
        out_specs=pl.BlockSpec(memory_space=pltpu.VMEM),
        scratch_shapes=[
            vmem((members, padded, rows), bf16),
            vmem((members, rows, padded), bf16),
            vmem((tokens, columns), bf16),
            vmem((rows, columns), f32),
            vmem((rows, columns), f32),
            vmem((chunks, members) + block, bf16),
            vmem((chunks, tokens, LANES), f32),
            vmem((chunks, padded, LANES), bf16),
            vmem((chunks, SIDE) + block, bf16),
            vmem((chunks, SIDE) + block, bf16),
            vmem((chunks, SIDE) + block, f32),
            vmem((chunks, SIDE) + block, bf16),
            vmem((chunks, SIDE) + block, bf16),
            vmem((chunks, SIDE) + block, bf16),
            vmem((chunks, SIDE) + block, bf16),
            vmem((chunks, SIDE) + block, f32),
            vmem((chunks,) + block, bf16),
            vmem((chunks, 2, rows // 2, LANES), bf16),
            vmem((chunks,) + block, bf16),
            vmem((chunks,) + block, bf16),
            vmem((chunks,) + block, bf16),
            vmem((chunks,) + block, bf16),
            vmem((chunks,) + block, f32),
            vmem((chunks,) + block, bf16),
            vmem((chunks,) + block, bf16),
            vmem((8, LANES), f32),
            vmem((2, members, 1, LANES), f32),
            dma((members + chunks + 1,)),
            dma((chunks, 16)),
            dma((chunks, 16)),
            dma((chunks, 16)),
            dma((chunks, 16)),
            dma((chunks + 1,)),
            dma((chunks + 1,)),
            dma((2, members)),
            dma((2, members)),
        ],
        compiler_params=pltpu.CompilerParams(
            collective_id=0, has_side_effects=True, vmem_limit_bytes=60 * 2**20
        ),
    )(activations[0], targets[0], weights[0], lengths[0])
    return averaged[None]


def solution(mesh):
    return jax.shard_map(
        local,
        mesh=mesh,
        in_specs=(
            P("replica", "fsdp", None),
            P("replica", "fsdp", None),
            P("replica", "fsdp", None),
            P("replica", None),
        ),
        out_specs=P("replica", "fsdp", None),
        check_vma=False,
    )
```

time: 114 us -> 98.6 us (0.86)
  Pallas kernels: 112 us -> 95.4 us
    pallas_call x1, Pallas kernels: 112 us -> 95.4 us  [local(): pl.pallas_call(functools.partial(kernel, bit), out_shape=jax.ShapeDtypeSt...]
where the time goes in v2:
time: 98.6 us; the launch traced here: 97.2 us
  Pallas kernels  95.4 us (97%)
  local copies, waits for them, and re-layouts  1.87 us (2%)
    pallas_call x1, Pallas kernels, local(): pl.pallas_call(functools.partial(kernel, bit), out_shape=jax.ShapeDtypeSt...  95.4 us

profile of v2, /device:TPU:6, one launch (start us, length us, event | category | flops | bytes accessed | tf_op | source)
XLA Modules:
  0.0 97.2 jit_solution(17030476961858380035)
XLA Ops:
  0.0 95.4 %shard_map.46 = f32[256,512]{1,0:T(8,128)} custom-call(bf16[448,4096]{1,0:T(8,128)(2,1)} %bitcast.5, bf16[448,512]{1,0:T(8,128)(2,1)} %bitcast.8, f32[256,512]{1,0:T(8,128)} %bitcast.7, s32[112]{0:T(128)} %bitcast.9), custom_call_target="tpu_custom_call" | custom-call | tf_op jit(solution)/shard_map/pallas_call | solution.py:515
  95.4 1.9 %copy.6 = f32[1,256,512]{2,1,0:T(8,128)} copy(f32[1,256,512]{2,1,0:T(8,128)} %bitcast.6) | data formatting | bytes 1048576

commit v3 on v2

--- a/solution.py
+++ b/solution.py
@@ -142,12 +142,6 @@
     def cut(c):
         return pl.ds(c * LANES, LANES)
 
-    load_w = []
-    for c in sorted(range(chunks), key=[o[1] for o in ORDER if o[0] == START].index):
-        load_w.append(
-            pltpu.make_async_copy(wgt.at[:, cut(c)], wm.at[:, cut(c)], load_sem.at[members + 1 + c])
-        )
-        load_w[-1].start()
     barrier = pltpu.get_barrier_semaphore()
     peer_y = {"replica": partner}
     for peer in (
@@ -158,6 +152,12 @@
         peer_y,
     ):
         pl.semaphore_signal(barrier, inc=1, device_id=peer, device_id_type=MESH)
+    load_w = {}
+    for c in sorted(range(chunks), key=[o[1] for o in ORDER if o[0] == START].index):
+        load_w[c] = pltpu.make_async_copy(
+            wgt.at[:, cut(c)], wm.at[:, cut(c)], load_sem.at[members + 1 + c]
+        )
+        load_w[c].start()
     load_a = []
     for m in range(members):
         load_a.append(
@@ -170,10 +170,12 @@
         load_a[-1].start()
     load_t = pltpu.make_async_copy(tgt, t_v, load_sem.at[members])
     load_t.start()
-    for c in range(chunks):
+
+    def round_rows(c):
         load_w[c].wait()
-    for c in range(chunks):
         w_all[c, fs] = wm[:, cut(c)].astype(jnp.bfloat16)
+
+    round_rows(ORDER[0][1])
     pl.semaphore_wait(barrier, 5)
 
     sent = []
@@ -474,6 +476,9 @@
         steps[name](c, which)
         starts += name == START
         if name == START and starts == 1:
+            for other in range(chunks):
+                if other != c:
+                    round_rows(other)
             send(wm, wp, y_s.at[chunks], y_r.at[chunks], peer_y)
 
     entries = depth * LANES * chunks

time: 98.6 us -> 98.5 us (level); the launches traced: 97.2 us -> 98.3 us
  Pallas kernels: 95.4 us -> 96.4 us
    pallas_call x1, Pallas kernels: 95.4 us -> 96.4 us  [local(): pl.pallas_call(functools.partial(kernel, bit), out_shape=jax.ShapeDtypeSt...]
where the time goes in v3:
time: 98.5 us; the launch traced here: 98.3 us
  Pallas kernels  96.4 us (98%)
  local copies, waits for them, and re-layouts  1.87 us (2%)
    pallas_call x1, Pallas kernels, local(): pl.pallas_call(functools.partial(kernel, bit), out_shape=jax.ShapeDtypeSt...  96.4 us

profile of v3, /device:TPU:6, one launch (start us, length us, event | category | flops | bytes accessed | tf_op | source)
XLA Modules:
  0.0 98.3 jit_solution(7354937179532472983)
XLA Ops:
  0.0 96.4 %shard_map.46 = f32[256,512]{1,0:T(8,128)} custom-call(bf16[448,4096]{1,0:T(8,128)(2,1)} %bitcast.5, bf16[448,512]{1,0:T(8,128)(2,1)} %bitcast.8, f32[256,512]{1,0:T(8,128)} %bitcast.7, s32[112]{0:T(128)} %bitcast.9), custom_call_target="tpu_custom_call" | custom-call | tf_op jit(solution)/shard_map/pallas_call | solution.py:520
  96.4 1.9 %copy.6 = f32[1,256,512]{2,1,0:T(8,128)} copy(f32[1,256,512]{2,1,0:T(8,128)} %bitcast.6) | data formatting | bytes 1048576

commit v4 on v2

--- a/solution.py
+++ b/solution.py
@@ -473,7 +473,7 @@
     for name, c, which in ORDER:
         steps[name](c, which)
         starts += name == START
-        if name == START and starts == 1:
+        if name == START and starts == chunks:
             send(wm, wp, y_s.at[chunks], y_r.at[chunks], peer_y)
 
     entries = depth * LANES * chunks

time: 98.6 us -> 98.2 us (level)
  no operation moved by 1% of the time
where the time goes in v4:
time: 98.2 us; the launch traced here: 97.2 us
  Pallas kernels  95.4 us (97%)
  local copies, waits for them, and re-layouts  1.87 us (2%)
    pallas_call x1, Pallas kernels, local(): pl.pallas_call(functools.partial(kernel, bit), out_shape=jax.ShapeDtypeSt...  95.4 us

profile of v4, /device:TPU:6, one launch (start us, length us, event | category | flops | bytes accessed | tf_op | source)
XLA Modules:
  0.0 97.2 jit_solution(6375818549071929616)
XLA Ops:
  0.0 95.4 %shard_map.46 = f32[256,512]{1,0:T(8,128)} custom-call(bf16[448,4096]{1,0:T(8,128)(2,1)} %bitcast.5, bf16[448,512]{1,0:T(8,128)(2,1)} %bitcast.8, f32[256,512]{1,0:T(8,128)} %bitcast.7, s32[112]{0:T(128)} %bitcast.9), custom_call_target="tpu_custom_call" | custom-call | tf_op jit(solution)/shard_map/pallas_call | solution.py:515
  95.4 1.9 %copy.6 = f32[1,256,512]{2,1,0:T(8,128)} copy(f32[1,256,512]{2,1,0:T(8,128)} %bitcast.6) | data formatting | bytes 1048576
